TPU v7x, 32 devices: a whole 2x2x4 slice. The times are simulated.
32 devices in a mesh: dp: 4 (over z), seq: 2 (over y), mp: 4 (over x, core).
Axes of the slice: x: 2, y: 2, z: 4, core: 2. Of those that a mesh axis runs over, the one named last changes fastest.
Arguments:
- hidden_in: bfloat16 [4, 1024, 768], P('dp', 'seq', 'mp'), may hold values from -6 to 6
- cotangent: bfloat16 [4, 1024, 768], P('dp', 'seq', 'mp'), may hold values from -6 to 6
- attention_gain: float32 [768], replicated, may hold values from 0.1 to 1.9
- feedforward_gain: float32 [768], replicated, may hold values from 0.1 to 1.9
- qkv_weight: bfloat16 [768, 3, 768], P(None, None, 'mp'), may hold values from -0.21875 to 0.21875
- attention_out: bfloat16 [768, 768], P('mp'), may hold values from -0.75 to 0.75
- geglu_in: bfloat16 [768, 2, 1152], P(None, None, 'mp'), may hold values from -0.21875 to 0.21875
- geglu_out: bfloat16 [1152, 768], P('mp'), may hold values from -0.1875 to 0.1875
Outputs:
- layer_out: float32 [4, 1024, 768], P('dp', 'seq', 'mp')
- grad_input: float32 [4, 1024, 768], P('dp', 'seq', 'mp')
- grad_qkv: float32 [768, 3, 768], P(None, None, 'mp')
- grad_attention_out: float32 [768, 768], P('mp')
- grad_geglu_in: float32 [768, 2, 1152], P(None, None, 'mp')
- grad_geglu_out: float32 [1152, 768], P('mp')
- grad_attention_gain: float32 [768], P('mp')
- grad_feedforward_gain: float32 [768], P('mp')
All inputs are finite; a program needn't handle non-finite values.
Results may differ from a plain program's by a relative error of at most 0.018.
Values may be sent and summed in bfloat16 or wider, within the bound.
No kernel may reach another device: no remote copies, remote signals or barrier semaphores. Data moves between devices by JAX's collectives and lax.ppermute only.
A program may use at most 64 MiB of HBM per device.

v0:
```python
import math
import jax
import jax.numpy as jnp
from jax import lax
from jax.sharding import PartitionSpec as P

HEAD = 64
HALF = 64


def with_halo(block, sides, width):
    for axis, dim in sides:
        count = lax.axis_size(axis)
        forward = [(i, i + 1) for i in range(count - 1)]
        backward = [(target, source) for source, target in forward]
        low = lax.ppermute(
            lax.slice_in_dim(block, block.shape[dim] - width, None, axis=dim), axis, forward
        )
        high = lax.ppermute(lax.slice_in_dim(block, 0, width, axis=dim), axis, backward)
        block = jnp.concatenate([low, block, high], axis=dim)
    return block


def normalize(rows):
    center = rows - jnp.mean(rows, axis=-1, keepdims=True)
    inverse = lax.rsqrt(jnp.mean(center * center, axis=-1, keepdims=True) + 1e-05)
    return (center * inverse, inverse)


def frequencies(positions):
    inverse_freq = jnp.exp(
        jnp.arange(HEAD // 2).astype(jnp.float32) * (-2.0 * math.log(10000.0) / HEAD)
    )
    angles = positions[:, None] * inverse_freq[None, :]
    angles = jnp.concatenate([angles, angles], axis=-1)
    return (jnp.cos(angles), jnp.sin(angles))


def rotate(tensor, cosine, sine):
    halfway = HEAD // 2
    turned = jnp.concatenate([-tensor[..., halfway:], tensor[..., :halfway]], axis=-1)
    return tensor * cosine[:, None, :] + turned * sine[:, None, :]


def gelu_exact(value):
    return 0.5 * value * (1.0 + lax.erf(value * 0.7071067811865476))


def gelu_slope(value):
    return (
        0.5 * (1.0 + lax.erf(value * 0.7071067811865476))
        + value * jnp.exp(-0.5 * value * value) * 0.3989422804014327
    )


def windows(wide, tile):
    count = (wide.shape[1] - tile) // tile
    shape = (wide.shape[0], count, tile) + wide.shape[2:]
    lower = wide[:, : count * tile].reshape(shape)
    upper = wide[:, tile:].reshape(shape)
    return jnp.concatenate([lower, upper], axis=2)


def unwindow(grads, tile):
    rest = grads.shape[3:]
    shape = (grads.shape[0], grads.shape[1] * tile) + rest
    lower = grads[:, :, :tile].reshape(shape)
    upper = grads[:, :, tile:].reshape(shape)
    others = ((0, 0),) * len(rest)
    return jnp.pad(lower, ((0, 0), (0, tile)) + others) + jnp.pad(
        upper, ((0, 0), (tile, 0)) + others
    )


def band_mask(base, count, tile, total_length):
    query_off = jnp.arange(tile, dtype=jnp.int32)
    key_off = jnp.arange(2 * tile, dtype=jnp.int32) - HALF
    near = jnp.abs(query_off[:, None] - key_off[None, :]) <= HALF
    key_pos = (
        base
        - HALF
        + jnp.arange(count, dtype=jnp.int32)[:, None] * tile
        + jnp.arange(2 * tile, dtype=jnp.int32)[None, :]
    )
    inside = (key_pos >= 0) & (key_pos < total_length)
    return near[None] & inside[:, None, :]


def attend(queries, keys_wide, values_wide, allowed):
    batch, length, heads, size = queries.shape
    tile = 2 * HALF
    count = length // tile
    query_tiles = queries.reshape(batch, count, tile, heads, size)
    key_tiles = windows(keys_wide, tile)
    value_tiles = windows(values_wide, tile)
    scores = jnp.einsum(
        "snqhd,snkhd->snhqk", query_tiles, key_tiles, preferred_element_type=jnp.float32
    ) * HEAD ** (-0.5)
    scores = jnp.where(allowed[None, :, None], scores, -1e30)
    top = jnp.max(scores, axis=-1, keepdims=True)
    log_total = top + jnp.log(jnp.sum(jnp.exp(scores - top), axis=-1, keepdims=True))
    weights = jnp.exp(scores - log_total).astype(jnp.bfloat16)
    mixed = jnp.einsum(
        "snhqk,snkhd->snqhd", weights, value_tiles, preferred_element_type=jnp.float32
    ).astype(jnp.bfloat16)
    return (mixed.reshape(batch, length, heads, size), log_total)


def attend_back(queries, keys_wide, values_wide, allowed, log_total, mixed, grad_mixed):
    batch, length, heads, size = queries.shape
    tile = 2 * HALF
    count = length // tile
    query_tiles = queries.reshape(batch, count, tile, heads, size)
    key_tiles = windows(keys_wide, tile)
    value_tiles = windows(values_wide, tile)
    grad_tiles = grad_mixed.reshape(batch, count, tile, heads, size)
    again = jnp.einsum(
        "snqhd,snkhd->snhqk", query_tiles, key_tiles, preferred_element_type=jnp.float32
    ) * HEAD ** (-0.5)
    again = jnp.where(allowed[None, :, None], again, -1e30)
    probs = jnp.exp(again - log_total)
    delta = jnp.sum(grad_mixed.astype(jnp.float32) * mixed.astype(jnp.float32), axis=-1)
    delta = jnp.transpose(delta.reshape(batch, count, tile, heads), (0, 1, 3, 2))
    grad_value_tiles = jnp.einsum(
        "snhqk,snqhd->snkhd",
        probs.astype(jnp.bfloat16),
        grad_tiles,
        preferred_element_type=jnp.float32,
    )
    grad_probs = jnp.einsum(
        "snqhd,snkhd->snhqk", grad_tiles, value_tiles, preferred_element_type=jnp.float32
    )
    grad_scores = (probs * (grad_probs - delta[..., None]) * HEAD ** (-0.5)).astype(jnp.bfloat16)
    grad_queries = jnp.einsum(
        "snhqk,snkhd->snqhd", grad_scores, key_tiles, preferred_element_type=jnp.float32
    )
    grad_key_tiles = jnp.einsum(
        "snhqk,snqhd->snkhd", grad_scores, query_tiles, preferred_element_type=jnp.float32
    )
    return (
        grad_queries.reshape(batch, length, heads, size),
        unwindow(grad_key_tiles, tile),
        unwindow(grad_value_tiles, tile),
    )


def edge_rims(grad_packed, length):
    return jnp.concatenate([grad_packed[:, :HALF], grad_packed[:, HALF + length :]], axis=1)


def fold_rims(grad_packed, returned, length):
    lower_add = jnp.pad(returned[:, :HALF], ((0, 0), (0, length - HALF), (0, 0)))
    upper_add = jnp.pad(returned[:, 3 * HALF :], ((0, 0), (length - HALF, 0), (0, 0)))
    return grad_packed[:, HALF : HALF + length] + lower_add + upper_add


def body(
    hidden_in,
    cotangent,
    attention_gain,
    feedforward_gain,
    qkv_weight,
    attention_out,
    geglu_in,
    geglu_out,
):
    batch, length, share = hidden_in.shape
    width = share * lax.axis_size("mp")
    offset = lax.axis_index("mp") * share
    columns = qkv_weight.shape[2]
    heads = columns // HEAD
    span = length + 2 * HALF
    inputs_full, upstream_full = (
        lax.all_gather(hidden_in, "mp", axis=2, tiled=True),
        lax.all_gather(cotangent, "mp", axis=2, tiled=True),
    )
    normed_one, inverse_one = normalize(inputs_full.astype(jnp.float32))
    fed_one = (normed_one * attention_gain).astype(jnp.bfloat16)
    projected = jnp.einsum("std,dch->stch", fed_one, qkv_weight, preferred_element_type=jnp.float32)
    block_index = lax.axis_index("seq")
    total_length = length * lax.axis_size("seq")
    query_pos = block_index * length + jnp.arange(length, dtype=jnp.int32)
    cosine, sine = frequencies(query_pos.astype(jnp.float32))
    queries = rotate(projected[:, :, 0].reshape(batch, length, heads, HEAD), cosine, sine).astype(
        jnp.bfloat16
    )
    keys_own = rotate(projected[:, :, 1].reshape(batch, length, heads, HEAD), cosine, sine).astype(
        jnp.bfloat16
    )
    values_own = projected[:, :, 2].astype(jnp.bfloat16)
    packed = jnp.concatenate([keys_own.reshape(batch, length, columns), values_own], axis=2)
    widened = with_halo(packed, (("seq", 1),), HALF)
    keys_wide = widened[:, :, :columns].reshape(batch, span, heads, HEAD)
    values_wide = widened[:, :, columns:].reshape(batch, span, heads, HEAD)
    allowed = band_mask(block_index * length, length // (2 * HALF), 2 * HALF, total_length)
    mixed, log_total = attend(queries, keys_wide, values_wide, allowed)
    joined = mixed.reshape(batch, length, columns)
    attn_terms = jnp.einsum(
        "sqh,hd->sqd", joined, attention_out, preferred_element_type=jnp.float32
    )
    middle = hidden_in.astype(jnp.float32) + lax.psum_scatter(
        attn_terms, "mp", scatter_dimension=2, tiled=True
    )
    middle_full = lax.all_gather(middle, "mp", axis=2, tiled=True)
    normed_two, inverse_two = normalize(middle_full)
    fed_two = (normed_two * feedforward_gain).astype(jnp.bfloat16)
    lifted = jnp.einsum("std,dcf->stcf", fed_two, geglu_in, preferred_element_type=jnp.float32)
    linear = lifted[:, :, 0]
    gating = lifted[:, :, 1]
    activated = gelu_exact(linear)
    product = (activated * gating).astype(jnp.bfloat16)
    mlp_terms = jnp.einsum("stf,fd->std", product, geglu_out, preferred_element_type=jnp.float32)
    layer_out = middle + lax.psum_scatter(
        mlp_terms.astype(jnp.bfloat16), "mp", scatter_dimension=2, tiled=True
    ).astype(jnp.float32)
    grad_geglu_out = jnp.einsum(
        "stf,std->fd", product, upstream_full, preferred_element_type=jnp.float32
    )
    grad_product = jnp.einsum(
        "std,fd->stf", upstream_full, geglu_out, preferred_element_type=jnp.float32
    )
    grad_linear = grad_product * gating * gelu_slope(linear)
    grad_gating = grad_product * activated
    grad_lifted = jnp.stack([grad_linear, grad_gating], axis=2).astype(jnp.bfloat16)
    grad_geglu_in = jnp.einsum(
        "std,stcf->dcf", fed_two, grad_lifted, preferred_element_type=jnp.float32
    )
    fed_terms = jnp.einsum(
        "stcf,dcf->std", grad_lifted, geglu_in, preferred_element_type=jnp.float32
    )
    grad_fed_two = lax.psum_scatter(fed_terms, "mp", scatter_dimension=2, tiled=True)
    normed_two_own = lax.dynamic_slice_in_dim(normed_two, offset, share, 2)
    gain_two_own = lax.dynamic_slice_in_dim(feedforward_gain, offset, share, 0)
    grad_ff_gain = jnp.sum(grad_fed_two * normed_two_own, axis=(0, 1))
    dhat_two = grad_fed_two * gain_two_own
    first_two, second_two = lax.psum(
        (
            jnp.sum(dhat_two, axis=-1, keepdims=True),
            jnp.sum(dhat_two * normed_two_own, axis=-1, keepdims=True),
        ),
        "mp",
    )
    grad_middle = cotangent.astype(jnp.float32) + inverse_two * (
        dhat_two - first_two / width - normed_two_own * (second_two / width)
    )
    grad_middle_full = lax.all_gather(grad_middle.astype(jnp.bfloat16), "mp", axis=2, tiled=True)
    grad_attention_out = jnp.einsum(
        "sqh,sqd->hd", joined, grad_middle_full, preferred_element_type=jnp.float32
    )
    grad_mixed = jnp.einsum(
        "sqd,hd->sqh", grad_middle_full, attention_out, preferred_element_type=jnp.float32
    ).astype(jnp.bfloat16)
    grad_mixed = grad_mixed.reshape(batch, length, heads, HEAD)
    grad_queries, grad_keys_wide, grad_values_wide = attend_back(
        queries, keys_wide, values_wide, allowed, log_total, mixed, grad_mixed
    )
    grad_packed = jnp.concatenate(
        [
            grad_keys_wide.reshape(batch, span, columns),
            grad_values_wide.reshape(batch, span, columns),
        ],
        axis=2,
    )
    returned = with_halo(
        edge_rims(grad_packed, length).astype(jnp.bfloat16), (("seq", 1),), HALF
    ).astype(jnp.float32)
    grad_own = fold_rims(grad_packed, returned, length)
    grad_keys = rotate(grad_own[:, :, :columns].reshape(batch, length, heads, HEAD), cosine, -sine)
    grad_queries = rotate(grad_queries, cosine, -sine)
    grad_values = grad_own[:, :, columns:].reshape(batch, length, heads, HEAD)
    grad_projected = (
        jnp.stack([grad_queries, grad_keys, grad_values], axis=2)
        .reshape(batch, length, 3, columns)
        .astype(jnp.bfloat16)
    )
    grad_qkv = jnp.einsum(
        "std,stch->dch", fed_one, grad_projected, preferred_element_type=jnp.float32
    )
    one_terms = jnp.einsum(
        "stch,dch->std", grad_projected, qkv_weight, preferred_element_type=jnp.float32
    )
    grad_fed_one = lax.psum_scatter(
        one_terms.astype(jnp.bfloat16), "mp", scatter_dimension=2, tiled=True
    ).astype(jnp.float32)
    normed_one_own = lax.dynamic_slice_in_dim(normed_one, offset, share, 2)
    gain_one_own = lax.dynamic_slice_in_dim(attention_gain, offset, share, 0)
    grad_attn_gain = jnp.sum(grad_fed_one * normed_one_own, axis=(0, 1))
    dhat_one = grad_fed_one * gain_one_own
    first_one, second_one = lax.psum(
        (
            jnp.sum(dhat_one, axis=-1, keepdims=True),
            jnp.sum(dhat_one * normed_one_own, axis=-1, keepdims=True),
        ),
        "mp",
    )
    grad_input = grad_middle + inverse_one * (
        dhat_one - first_one / width - normed_one_own * (second_one / width)
    )
    local_grads = (
        grad_qkv,
        grad_attention_out,
        grad_geglu_in,
        grad_geglu_out,
        grad_attn_gain,
        grad_ff_gain,
    )
    summed = lax.psum(
        (
            local_grads[0],
            local_grads[1],
            local_grads[2],
            local_grads[3],
            local_grads[4],
            local_grads[5],
        ),
        ("dp", "seq"),
    )
    return (layer_out, grad_input, summed[0], summed[1], summed[2], summed[3], summed[4], summed[5])


def solution(mesh):
    in_specs = (
        P("dp", "seq", "mp"),
        P("dp", "seq", "mp"),
        P(),
        P(),
        P(None, None, "mp"),
        P("mp", None),
        P(None, None, "mp"),
        P("mp", None),
    )
    out_specs = (
        P("dp", "seq", "mp"),
        P("dp", "seq", "mp"),
        P(None, None, "mp"),
        P("mp", None),
        P(None, None, "mp"),
        P("mp", None),
        P("mp"),
        P("mp"),
    )
    return jax.shard_map(body, mesh=mesh, in_specs=in_specs, out_specs=out_specs, check_vma=False)
```

profile of v0, /device:TPU:0, one launch (start us, length us, event | category | flops | bytes accessed | tf_op | source)
XLA Modules:
  0.0 433.2 jit_solution(13001490404904794870)
XLA Ops:
  7.3 10.4 %all_gather.12 = bf16[1,512,768]{1,2,0:T(8,128)(2,1)S(1)} all-gather(bf16[1,512,192]{1,2,0:T(8,128)(2,1)} %param.8), channel_id=1, replica_groups=mesh['dp'=4,'seq'=2,'mp'=4] {'mp'}, dimensions={2}, use_global_device_ids=true | all-gather | bytes 983040 | tf_op jit(solution)/shard_map/all_gather | solution.py:174
  22.8 3.4 collective-permute-start
  37.7 2.7 copy.56
  42.3 43.4 %all-reduce.16.cloned.1.call-done = f32[1,512,768]{1,0,2:T(1,128)} async-done(((f32[1,512,768]{1,0,2:T(1,128)}), f32[1,512,768]{1,0,2:T(1,128)}) %all-reduce.16.cloned.1.call-update) | async-done | bytes 1572880
  87.9 8.6 %all_gather.14 = bf16[1,512,768]{1,2,0:T(8,128)(2,1)} all-gather(bf16[1,512,192]{1,2,0:T(8,128)(2,1)S(1)} %copy-done.12), channel_id=1, replica_groups=mesh['dp'=4,'seq'=2,'mp'=4] {'mp'}, dimensions={2}, use_global_device_ids=true | all-gather | bytes 983040 | tf_op jit(solution)/shard_map/all_gather | solution.py:175
  96.5 11.2 %all-gather.2.cloned.1.call-done = f32[1,512,768]{1,0,2:T(1,128)} async-done(((f32[1,512,192]{1,0,2:T(1,128)}), f32[1,512,768]{1,0,2:T(1,128)}) %all-gather.2.cloned.1.call-update) | async-done | bytes 1572880 | tf_op jit(solution)/shard_map/all_gather | solution.py:204
  107.7 2.4 reduce_sum.111
  117.8 4.8 %copy.60 = f32[1,512,768]{1,0,2:T(1,128)} copy(f32[1,512,768]{2,1,0:T(8,128)} %convolution_bitcast_fusion) | data formatting | bytes 3145728 | tf_op jit(solution)/shard_map/stcf,dcf->std/dot_general | solution.py:228
  123.6 2.9 fusion.6
  126.6 4.8 %copy.86 = bf16[1,512,768]{1,0,2:T(2,128)(2,1)} copy(bf16[1,512,768]{2,1,0:T(8,128)(2,1)} %fusion.6) | data formatting | bytes 1572864
  131.3 2.5 copy.151
  133.9 31.7 %all-reduce.18.cloned.1.call-done = f32[1,512,768]{1,0,2:T(1,128)} async-done(((f32[1,512,768]{1,0,2:T(1,128)}), f32[1,512,768]{1,0,2:T(1,128)}) %all-reduce.18.cloned.1.call-update) | async-done | bytes 1572880
  167.8 6.0 %all-reduce.11 = (f32[1,512,1]{1,2,0:T(1,128)S(1)}, f32[1,512,1]{1,2,0:T(1,128)S(1)}) all-reduce(f32[1,512,1]{1,2,0:T(1,128)S(1)} %bitcast.303, f32[1,512,1]{1,2,0:T(1,128)S(1)} %bitcast.304), channel_id=1, replica_groups=mesh['dp'=4,'seq'=2,'mp'=4] {'mp'}, use_global_device_ids=true, to_apply=%region_12.13 | all-reduce | flops 1024 | bytes 8192 | tf_op jit(solution)/shard_map/psum | solution.py:236
  175.0 8.3 %all_gather.15 = bf16[1,512,768]{1,2,0:T(8,128)(2,1)S(1)} all-gather(bf16[1,512,192]{1,2,0:T(8,128)(2,1)S(1)} %fusion.98), channel_id=1, replica_groups=mesh['dp'=4,'seq'=2,'mp'=4] {'mp'}, dimensions={2}, use_global_device_ids=true | all-gather | bytes 983040 | tf_op jit(solution)/shard_map/all_gather | solution.py:246
  193.4 3.4 collective-permute-start.2
  199.4 4.1 collective-permute-done.3
  207.9 4.8 %copy.88 = bf16[1,512,768]{1,0,2:T(2,128)(2,1)} copy(bf16[1,512,768]{2,1,0:T(8,128)(2,1)} %fusion.5) | data formatting | bytes 1572864
  212.6 2.5 copy.150
  215.2 2.9 fusion.16
  227.1 10.6 %reduce-scatter.9.cloned.1.call-done = bf16[192,512]{1,0:T(8,128)(2,1)} async-done(((bf16[768,512]{1,0:T(8,128)(2,1)}), bf16[192,512]{1,0:T(8,128)(2,1)}) %reduce-scatter.9.cloned.1.call-update) | async-done | bytes 196624
  240.0 22.6 %all-reduce.8 = (f32[192]{0:T(256)}, f32[192]{0:T(256)}) all-reduce(f32[192]{0:T(256)S(1)} %get-tuple-element.34, f32[192]{0:T(256)S(1)} %get-tuple-element.32), channel_id=1, replica_groups=mesh['dp'=4,'seq'=2,'mp'=4] {'dp','seq'}, use_global_device_ids=true, to_apply=%region_24.25 | all-reduce | flops 384 | bytes 3072 | tf_op jit(solution)/shard_map/psum | solution.py:307
  262.6 6.0 %all-reduce.10 = (f32[1,512,1]{1,2,0:T(1,128)S(1)}, f32[1,512,1]{1,2,0:T(1,128)S(1)}) all-reduce(f32[1,512,1]{1,2,0:T(1,128)S(1)} %bitcast.301, f32[1,512,1]{1,2,0:T(1,128)S(1)} %bitcast.302), channel_id=1, replica_groups=mesh['dp'=4,'seq'=2,'mp'=4] {'mp'}, use_global_device_ids=true, to_apply=%region_18.19 | all-reduce | flops 1024 | bytes 8192 | tf_op jit(solution)/shard_map/psum | solution.py:289
  270.7 149.2 %all-reduce.20.cloned.1.call-done = (f32[768,3,192]{0,2,1:T(8,128)}, f32[192,768]{1,0:T(8,128)}, f32[768,2,288]{0,2,1:T(8,128)}, f32[288,768]{1,0:T(8,128)}) async-done(((f32[768,3,192]{0,2,1:T(8,128)}, f32[192,768]{1,0:T(8,128)}, f32[768,2,288]{0,2,1:T(8,128)}, f32[288,768]{1,0:T(8,128)}), (f32[768,3,192]{0,2,1:T(8,128)}, f32[192,768]{1,0:T(8,128)}, f32[768,2,288]{0,2,1:T(8,128)}, ...) | async-done | bytes 5013520 | tf_op jit(solution)/shard_map/psum | solution.py:307
  419.9 2.9 copy.158
  (227 shorter events, 65.4 us)
Async XLA Ops:
  7.2 10.9 %copy-start = (bf16[768,3,192]{0,2,1:T(8,128)(2,1)S(1)}, bf16[768,3,192]{0,2,1:T(8,128)(2,1)}, u32[]{:S(2)}) copy-start(bf16[768,3,192]{0,2,1:T(8,128)(2,1)} %param.12) | copy-start | bytes 2654212
  7.2 10.9 %copy-start.47 = (f32[768]{0:T(1024)S(1)}, f32[768]{0:T(1024)}, u32[]{:S(2)}) copy-start(f32[768]{0:T(1024)} %param.10) | copy-start | bytes 9220
  7.2 78.5 %all-reduce.16.cloned.1.call-start = ((), (), s32[]{:S(2)}) async-start(), calls=%async_computation.5 | async-start | bytes 3145728
  22.8 9.8 %collective-permute-start = (bf16[1,64,384]{1,2,0:T(8,128)(2,1)}, bf16[1,64,384]{1,2,0:T(8,128)(2,1)S(1)}, u32[]{:S(2)}, u32[]{:S(2)}) collective-permute-start(bf16[1,64,384]{1,2,0:T(8,128)(2,1)} %get-tuple-element.71), channel_id=1, source_target_pairs={{0,4},{1,5},{2,6},{3,7},{8,12},{9,13},{10,14},{11,15},{16,20},{17,... | collective-permute-start | bytes 147464 | tf_op jit(solution)/shard_map/ppermute | solution.py:16
  26.2 6.8 %collective-permute-start.1 = (bf16[1,64,384]{1,2,0:T(8,128)(2,1)S(1)}, bf16[1,64,384]{1,2,0:T(8,128)(2,1)}, u32[]{:S(2)}, u32[]{:S(2)}) collective-permute-start(bf16[1,64,384]{1,2,0:T(8,128)(2,1)S(1)} %get-tuple-element.72), channel_id=1, source_target_pairs={{4,0},{5,1},{6,2},{7,3},{12,8},{13,9},{14,10},{15,11},{20,16},{21,... | collective-permute-start | bytes 147464 | tf_op jit(solution)/shard_map/ppermute | solution.py:19
  40.4 45.3 %copy-start.35 = (bf16[1,512,192]{1,2,0:T(8,128)(2,1)S(1)}, bf16[1,512,192]{1,2,0:T(8,128)(2,1)}, u32[]{:S(2)}) copy-start(bf16[1,512,192]{1,2,0:T(8,128)(2,1)} %param.8) | copy-start | bytes 589828
  40.4 47.5 %copy-start.12 = (bf16[1,512,192]{1,2,0:T(8,128)(2,1)S(1)}, bf16[1,512,192]{1,2,0:T(8,128)(2,1)}, u32[]{:S(2)}) copy-start(bf16[1,512,192]{1,2,0:T(8,128)(2,1)} %param.9) | copy-start | bytes 589828
  40.5 67.3 %all-gather.2.cloned.1.call-start = ((), (), s32[]{:S(2)}) async-start(), calls=%async_computation.2 | async-start | bytes 1966080 | tf_op jit(solution)/shard_map/all_gather | solution.py:204
  87.9 77.7 %all-reduce.18.cloned.1.call-start = ((), (), s32[]{:S(2)}) async-start(), calls=%async_computation.6 | async-start | bytes 3145728
  107.7 2.4 copy-start.3
  122.6 102.3 %reduce-scatter.7.cloned.1.call-start = ((), (), s32[]{:S(2)}) async-start(), calls=%async_computation.3 | async-start | bytes 983040
  133.8 40.0 %copy-start.13 = (bf16[1,512,192]{1,2,0:T(8,128)(2,1)S(1)}, bf16[1,512,192]{1,2,0:T(8,128)(2,1)}, u32[]{:S(2)}) copy-start(bf16[1,512,192]{1,2,0:T(8,128)(2,1)} %param.9) | copy-start | bytes 589828
  133.9 103.9 %reduce-scatter.9.cloned.1.call-start = ((), (), s32[]{:S(2)}) async-start(), calls=%async_computation.4 | async-start | bytes 983040
  173.8 10.4 %copy-start.21 = (bf16[192,768]{1,0:T(8,128)(2,1)S(1)}, bf16[192,768]{1,0:T(8,128)(2,1)}, u32[]{:S(2)}) copy-start(bf16[192,768]{1,0:T(8,128)(2,1)} %param.13) | copy-start | bytes 884740
  185.3 3.8 copy-start.26
  193.4 5.9 %collective-permute-start.2 = (bf16[1,64,384]{1,2,0:T(8,128)(2,1)S(1)}, bf16[1,64,384]{1,2,0:T(8,128)(2,1)S(1)}, u32[]{:S(2)}, u32[]{:S(2)}) collective-permute-start(bf16[1,64,384]{1,2,0:T(8,128)(2,1)S(1)} %get-tuple-element.53), channel_id=1, source_target_pairs={{0,4},{1,5},{2,6},{3,7},{8,12},{9,13},{10,14},{11,15},{16,20},{17,... | collective-permute-start | bytes 147464 | tf_op jit(solution)/shard_map/ppermute | solution.py:16
  196.8 6.7 %collective-permute-start.3 = (bf16[1,64,384]{1,2,0:T(8,128)(2,1)S(1)}, bf16[1,64,384]{1,2,0:T(8,128)(2,1)S(1)}, u32[]{:S(2)}, u32[]{:S(2)}) collective-permute-start(bf16[1,64,384]{1,2,0:T(8,128)(2,1)S(1)} %get-tuple-element.54), channel_id=1, source_target_pairs={{4,0},{5,1},{6,2},{7,3},{12,8},{13,9},{14,10},{15,11},{20,16},{21,... | collective-permute-start | bytes 147464 | tf_op jit(solution)/shard_map/ppermute | solution.py:19
  215.1 204.8 %all-reduce.20.cloned.1.call-start = ((), (), s32[]{:S(2)}) async-start(), calls=%async_computation.7 | async-start | bytes 10027008 | tf_op jit(solution)/shard_map/psum | solution.py:307
  215.2 2.9 copy-start.43
  215.2 2.9 copy-start.45
  224.9 43.8 %copy-start.8 = (f32[1,512,192]{1,0,2:T(1,128)S(1)}, f32[1,512,192]{1,0,2:T(1,128)}, u32[]{:S(2)}) copy-start(f32[1,512,192]{1,0,2:T(1,128)} %copy-done.7) | copy-start | bytes 1179652
  224.9 43.8 %copy-start.14 = (bf16[1,512,192]{1,2,0:T(8,128)(2,1)S(1)}, bf16[1,512,192]{1,2,0:T(8,128)(2,1)}, u32[]{:S(2)}) copy-start(bf16[1,512,192]{1,2,0:T(8,128)(2,1)} %param.9) | copy-start | bytes 589828
  419.9 3.0 copy-start.40
  419.9 3.8 copy-start.11
  (36 other events, 43.5 us)
Sparse Core Ops, SparseCore 0:
  40.6 45.0 all-reduce.15
  88.0 19.6 all-gather.1
  122.7 42.8 all-reduce.17
  168.0 23.2 reduce-scatter.6
  215.3 22.4 reduce-scatter.8
  242.1 177.7 all-reduce.19
where the time goes:
time: 434 us; the launch traced here: 433 us
  waiting for transfers between devices  251 us (58%)
  blocking collectives  61.9 us (14%)
  local copies, waits for them, and re-layouts  47.5 us (11%)
  other arithmetic  25.6 us (6%)
  matrix products  21.8 us (5%)
  between operations  15.6 us (4%)
  starting transfers between devices  9.63 us (2%)
    psum x1, waiting for transfers between devices, body(): lax.psum((local_grads[0], local_grads[1], local_grads[2], local_grads[3],...  149 us
    unnamed x10, waiting for transfers between devices  85.8 us
    unnamed x117, local copies, waits for them, and re-layouts  34.8 us
    psum x1, blocking collectives, body(): lax.psum((local_grads[0], local_grads[1], local_grads[2], local_grads[3],...  22.6 us
    all_gather x1, waiting for transfers between devices, body(): middle_full = lax.all_gather(middle, 'mp', axis=2, tiled=True)  11.2 us
    all_gather x1, blocking collectives, body(): lax.all_gather(hidden_in, 'mp', axis=2, tiled=True)  10.4 us
  transfers between devices with their start and end apart: 10, of which 8 were waited for; matrix products, arithmetic and copies ran while one was open for 13% of the time, Pallas kernels for 0%

commit v1 on v0

--- a/solution.py
+++ b/solution.py
@@ -304,7 +304,7 @@
         grad_attn_gain,
         grad_ff_gain,
     )
-    summed = lax.psum(
+    one_axis = lax.psum(
         (
             local_grads[0],
             local_grads[1],
@@ -313,8 +313,9 @@
             local_grads[4],
             local_grads[5],
         ),
-        ("dp", "seq"),
-    )
+        "dp",
+    )
+    summed = lax.psum(one_axis, "seq")
     return (layer_out, grad_input, summed[0], summed[1], summed[2], summed[3], summed[4], summed[5])
 
 

time: 434 us -> 580 us (1.34)
  waiting for transfers between devices: 251 us -> 405 us
    psum x0 -> x1, waiting for transfers between devices: none -> 101 us  [body(): summed = lax.psum(one_axis, 'seq')]
    unnamed x10 -> x11, waiting for transfers between devices: 85.8 us -> 125 us
    psum x1, waiting for transfers between devices: 149 us -> 160 us  [body(): lax.psum((local_grads[0], local_grads[1], local_grads[2], local_grads[3],...]
    psum x1, blocking collectives: 22.6 us -> 11.7 us  [body(): lax.psum((local_grads[0], local_grads[1], local_grads[2], local_grads[3],...]
    unnamed x117 -> x109, local copies, waits for them, and re-layouts: 34.8 us -> 33.3 us
  transfers between devices with their start and end apart: 10 -> 11, of which waited for: 8 -> 10; matrix products, arithmetic and copies ran while one was open for 13% -> 6% of each run, Pallas kernels for 0% -> 0%
where the time goes in v1:
time: 580 us; the launch traced here: 579 us
  waiting for transfers between devices  405 us (70%)
  blocking collectives  56.7 us (10%)
  local copies, waits for them, and re-layouts  45.1 us (8%)
  other arithmetic  23.3 us (4%)
  matrix products  22.9 us (4%)
  between operations  15.7 us (3%)
  starting transfers between devices  10.3 us (2%)
    psum x1, waiting for transfers between devices, body(): lax.psum((local_grads[0], local_grads[1], local_grads[2], local_grads[3],...  160 us
    unnamed x11, waiting for transfers between devices  125 us
    psum x1, waiting for transfers between devices, body(): summed = lax.psum(one_axis, 'seq')  101 us
    unnamed x109, local copies, waits for them, and re-layouts  33.3 us
    psum x1, blocking collectives, body(): lax.psum((local_grads[0], local_grads[1], local_grads[2], local_grads[3],...  11.7 us
  transfers between devices with their start and end apart: 11, of which 10 were waited for; matrix products, arithmetic and copies ran while one was open for 6% of the time, Pallas kernels for 0%

profile of v1, /device:TPU:0, one launch (start us, length us, event | category | flops | bytes accessed | tf_op | source)
XLA Modules:
  0.0 579.3 jit_solution(18368713442279737928)
XLA Ops:
  7.3 10.4 %all_gather.12 = bf16[1,512,768]{1,2,0:T(8,128)(2,1)S(1)} all-gather(bf16[1,512,192]{1,2,0:T(8,128)(2,1)} %param.8), channel_id=1, replica_groups=mesh['dp'=4,'seq'=2,'mp'=4] {'mp'}, dimensions={2}, use_global_device_ids=true | all-gather | bytes 983040 | tf_op jit(solution)/shard_map/all_gather | solution.py:174
  22.8 4.1 collective-permute-start
  30.1 3.8 collective-permute-done.1
  43.2 41.0 %all-reduce.19.cloned.1.call-done = f32[1,512,768]{1,0,2:T(1,128)} async-done(((f32[1,512,768]{1,0,2:T(1,128)}), f32[1,512,768]{1,0,2:T(1,128)}) %all-reduce.19.cloned.1.call-update) | async-done | bytes 1572880
  86.5 8.6 %all_gather.14 = bf16[1,512,768]{1,2,0:T(8,128)(2,1)} all-gather(bf16[1,512,192]{1,2,0:T(8,128)(2,1)S(1)} %copy-done.10), channel_id=1, replica_groups=mesh['dp'=4,'seq'=2,'mp'=4] {'mp'}, dimensions={2}, use_global_device_ids=true | all-gather | bytes 983040 | tf_op jit(solution)/shard_map/all_gather | solution.py:175
  95.1 11.2 %all-gather.2.cloned.1.call-done = f32[1,512,768]{1,0,2:T(1,128)} async-done(((f32[1,512,192]{1,0,2:T(1,128)}), f32[1,512,768]{1,0,2:T(1,128)}) %all-gather.2.cloned.1.call-update) | async-done | bytes 1572880 | tf_op jit(solution)/shard_map/all_gather | solution.py:204
  116.3 4.8 copy.60
  122.2 2.9 fusion.16
  127.0 37.1 %all-reduce.21.cloned.1.call-done = f32[1,512,768]{1,0,2:T(1,128)} async-done(((f32[1,512,768]{1,0,2:T(1,128)}), f32[1,512,768]{1,0,2:T(1,128)}) %all-reduce.21.cloned.1.call-update) | async-done | bytes 1572880
  166.4 6.0 %all-reduce.9 = (f32[1,512,1]{1,2,0:T(1,128)S(1)}, f32[1,512,1]{1,2,0:T(1,128)S(1)}) all-reduce(f32[1,512,1]{1,2,0:T(1,128)S(1)} %bitcast.303, f32[1,512,1]{1,2,0:T(1,128)S(1)} %bitcast.304), channel_id=1, replica_groups=mesh['dp'=4,'seq'=2,'mp'=4] {'mp'}, use_global_device_ids=true, to_apply=%region_12.13 | all-reduce | flops 1024 | bytes 8192 | tf_op jit(solution)/shard_map/psum | solution.py:236
  173.6 8.3 %all_gather.15 = bf16[1,512,768]{1,2,0:T(8,128)(2,1)S(1)} all-gather(bf16[1,512,192]{1,2,0:T(8,128)(2,1)S(1)} %fusion.98), channel_id=1, replica_groups=mesh['dp'=4,'seq'=2,'mp'=4] {'mp'}, dimensions={2}, use_global_device_ids=true | all-gather | bytes 983040 | tf_op jit(solution)/shard_map/all_gather | solution.py:246
  192.3 3.4 collective-permute-start.2
  198.3 4.1 collective-permute-done.3
  206.4 2.9 fusion.6
  209.4 4.8 copy.86
  219.6 4.8 copy.88
  227.0 160.3 %all-reduce.23.cloned.1.call-done = (f32[768,3,192]{0,2,1:T(8,128)}, f32[192,768]{1,0:T(8,128)}, f32[768,2,288]{0,2,1:T(8,128)}, f32[288,768]{1,0:T(8,128)}) async-done(((f32[768,3,192]{0,2,1:T(8,128)}, f32[192,768]{1,0:T(8,128)}, f32[768,2,288]{0,2,1:T(8,128)}, f32[288,768]{1,0:T(8,128)}), (f32[768,3,192]{0,2,1:T(8,128)}, f32[192,768]{1,0:T(8,128)}, f32[768,2,288]{0,2,1:T(8,128)}, ...) | async-done | bytes 5013520 | tf_op jit(solution)/shard_map/psum | solution.py:307
  388.8 23.1 %reduce-scatter.7.cloned.1.call-done = bf16[192,512]{1,0:T(8,128)(2,1)} async-done(((bf16[768,512]{1,0:T(8,128)(2,1)}), bf16[192,512]{1,0:T(8,128)(2,1)}) %reduce-scatter.7.cloned.1.call-update) | async-done | bytes 196624
  414.1 23.5 %reduce-scatter.9.cloned.1.call-done = bf16[192,512]{1,0:T(8,128)(2,1)} async-done(((bf16[768,512]{1,0:T(8,128)(2,1)}), bf16[192,512]{1,0:T(8,128)(2,1)}) %reduce-scatter.9.cloned.1.call-update) | async-done | bytes 196624
  439.9 11.7 %all-reduce.10 = (f32[192]{0:T(256)S(1)}, f32[192]{0:T(256)S(1)}) all-reduce(f32[192]{0:T(256)S(1)} %get-tuple-element.34, f32[192]{0:T(256)S(1)} %get-tuple-element.32), channel_id=1, replica_groups=mesh['dp'=4,'seq'=2,'mp'=4] {'dp'}, use_global_device_ids=true, to_apply=%region_28.29 | all-reduce | flops 384 | bytes 3072 | tf_op jit(solution)/shard_map/psum | solution.py:307
  451.5 5.7 all-reduce.12
  457.2 6.0 %all-reduce.8 = (f32[1,512,1]{1,2,0:T(1,128)S(1)}, f32[1,512,1]{1,2,0:T(1,128)S(1)}) all-reduce(f32[1,512,1]{1,2,0:T(1,128)S(1)} %bitcast.299, f32[1,512,1]{1,2,0:T(1,128)S(1)} %bitcast.300), channel_id=1, replica_groups=mesh['dp'=4,'seq'=2,'mp'=4] {'mp'}, use_global_device_ids=true, to_apply=%region_18.19 | all-reduce | flops 1024 | bytes 8192 | tf_op jit(solution)/shard_map/psum | solution.py:289
  465.3 100.6 %all-reduce.25.cloned.1.call-done = (f32[768,3,192]{0,2,1:T(8,128)}, f32[192,768]{1,0:T(8,128)}, f32[768,2,288]{0,2,1:T(8,128)}, f32[288,768]{1,0:T(8,128)}) async-done(((f32[768,3,192]{0,2,1:T(8,128)}, f32[192,768]{1,0:T(8,128)}, f32[768,2,288]{0,2,1:T(8,128)}, f32[288,768]{1,0:T(8,128)}), (f32[768,3,192]{0,2,1:T(8,128)}, f32[192,768]{1,0:T(8,128)}, f32[768,2,288]{0,2,1:T(8,128)}, ...) | async-done | bytes 5013520 | tf_op jit(solution)/shard_map/psum | solution.py:318
  566.0 2.9 copy.162
  (223 shorter events, 71.4 us)
Async XLA Ops:
  7.2 10.9 %copy-start = (bf16[768,3,192]{0,2,1:T(8,128)(2,1)S(1)}, bf16[768,3,192]{0,2,1:T(8,128)(2,1)}, u32[]{:S(2)}) copy-start(bf16[768,3,192]{0,2,1:T(8,128)(2,1)} %param.12) | copy-start | bytes 2654212
  7.2 10.9 %copy-start.43 = (f32[768]{0:T(1024)S(1)}, f32[768]{0:T(1024)}, u32[]{:S(2)}) copy-start(f32[768]{0:T(1024)} %param.10) | copy-start | bytes 9220
  7.2 77.0 %all-reduce.19.cloned.1.call-start = ((), (), s32[]{:S(2)}) async-start(), calls=%async_computation.5 | async-start | bytes 3145728
  22.8 7.3 %collective-permute-start = (bf16[1,64,384]{1,2,0:T(8,128)(2,1)}, bf16[1,64,384]{1,2,0:T(8,128)(2,1)}, u32[]{:S(2)}, u32[]{:S(2)}) collective-permute-start(bf16[1,64,384]{1,2,0:T(8,128)(2,1)} %get-tuple-element.77), channel_id=1, source_target_pairs={{0,4},{1,5},{2,6},{3,7},{8,12},{9,13},{10,14},{11,15},{16,20},{17,... | collective-permute-start | bytes 147464 | tf_op jit(solution)/shard_map/ppermute | solution.py:16
  26.9 7.0 %collective-permute-start.1 = (bf16[1,64,384]{1,2,0:T(8,128)(2,1)}, bf16[1,64,384]{1,2,0:T(8,128)(2,1)}, u32[]{:S(2)}, u32[]{:S(2)}) collective-permute-start(bf16[1,64,384]{1,2,0:T(8,128)(2,1)} %get-tuple-element.78), channel_id=1, source_target_pairs={{4,0},{5,1},{6,2},{7,3},{12,8},{13,9},{14,10},{15,11},{20,16},{21,... | collective-permute-start | bytes 147464 | tf_op jit(solution)/shard_map/ppermute | solution.py:19
  30.0 5.4 copy-start.22
  41.3 42.9 %copy-start.33 = (bf16[1,512,192]{1,2,0:T(8,128)(2,1)S(1)}, bf16[1,512,192]{1,2,0:T(8,128)(2,1)}, u32[]{:S(2)}) copy-start(bf16[1,512,192]{1,2,0:T(8,128)(2,1)} %param.8) | copy-start | bytes 589828
  41.3 45.1 %copy-start.10 = (bf16[1,512,192]{1,2,0:T(8,128)(2,1)S(1)}, bf16[1,512,192]{1,2,0:T(8,128)(2,1)}, u32[]{:S(2)}) copy-start(bf16[1,512,192]{1,2,0:T(8,128)(2,1)} %param.9) | copy-start | bytes 589828
  41.3 64.9 %all-gather.2.cloned.1.call-start = ((), (), s32[]{:S(2)}) async-start(), calls=%async_computation.2 | async-start | bytes 1966080 | tf_op jit(solution)/shard_map/all_gather | solution.py:204
  86.4 77.8 %all-reduce.21.cloned.1.call-start = ((), (), s32[]{:S(2)}) async-start(), calls=%async_computation.6 | async-start | bytes 3145728
  121.2 266.1 %all-reduce.23.cloned.1.call-start = ((), (), s32[]{:S(2)}) async-start(), calls=%async_computation.7 | async-start | bytes 10027008 | tf_op jit(solution)/shard_map/psum | solution.py:307
  121.2 3.9 copy-start.39
  121.2 3.9 copy-start.41
  127.0 45.3 %copy-start.11 = (bf16[1,512,192]{1,2,0:T(8,128)(2,1)S(1)}, bf16[1,512,192]{1,2,0:T(8,128)(2,1)}, u32[]{:S(2)}) copy-start(bf16[1,512,192]{1,2,0:T(8,128)(2,1)} %param.9) | copy-start | bytes 589828
  172.3 9.6 %copy-start.19 = (bf16[192,768]{1,0:T(8,128)(2,1)S(1)}, bf16[192,768]{1,0:T(8,128)(2,1)}, u32[]{:S(2)}) copy-start(bf16[192,768]{1,0:T(8,128)(2,1)} %param.13) | copy-start | bytes 884740
  172.3 9.9 %copy-start.14 = (bf16[1,4,128,3,64]{2,1,4,3,0:T(4,128)(2,1)S(1)}, bf16[1,4,128,3,64]{2,1,4,3,0:T(4,128)(2,1)}, u32[]{:S(2)}) copy-start(bf16[1,4,128,3,64]{2,1,4,3,0:T(4,128)(2,1)} %copy-done.13) | copy-start | bytes 589828
  184.2 3.8 copy-start.24
  192.3 5.9 %collective-permute-start.2 = (bf16[1,64,384]{1,2,0:T(8,128)(2,1)S(1)}, bf16[1,64,384]{1,2,0:T(8,128)(2,1)S(1)}, u32[]{:S(2)}, u32[]{:S(2)}) collective-permute-start(bf16[1,64,384]{1,2,0:T(8,128)(2,1)S(1)} %get-tuple-element.59), channel_id=1, source_target_pairs={{0,4},{1,5},{2,6},{3,7},{8,12},{9,13},{10,14},{11,15},{16,20},{17,... | collective-permute-start | bytes 147464 | tf_op jit(solution)/shard_map/ppermute | solution.py:16
  195.7 6.7 %collective-permute-start.3 = (bf16[1,64,384]{1,2,0:T(8,128)(2,1)S(1)}, bf16[1,64,384]{1,2,0:T(8,128)(2,1)S(1)}, u32[]{:S(2)}, u32[]{:S(2)}) collective-permute-start(bf16[1,64,384]{1,2,0:T(8,128)(2,1)S(1)} %get-tuple-element.60), channel_id=1, source_target_pairs={{4,0},{5,1},{6,2},{7,3},{12,8},{13,9},{14,10},{15,11},{20,16},{21,... | collective-permute-start | bytes 147464 | tf_op jit(solution)/shard_map/ppermute | solution.py:19
  206.4 205.5 %reduce-scatter.7.cloned.1.call-start = ((), (), s32[]{:S(2)}) async-start(), calls=%async_computation.3 | async-start | bytes 983040
  216.7 220.8 %reduce-scatter.9.cloned.1.call-start = ((), (), s32[]{:S(2)}) async-start(), calls=%async_computation.4 | async-start | bytes 983040
  226.9 339.0 %all-reduce.25.cloned.1.call-start = ((), (), s32[]{:S(2)}) async-start(), calls=%async_computation.8 | async-start | bytes 10027008 | tf_op jit(solution)/shard_map/psum | solution.py:318
  388.8 74.5 %copy-start.6 = (f32[1,512,192]{1,0,2:T(1,128)S(1)}, f32[1,512,192]{1,0,2:T(1,128)}, u32[]{:S(2)}) copy-start(f32[1,512,192]{1,0,2:T(1,128)} %copy-done.5) | copy-start | bytes 1179652
  388.8 74.5 %copy-start.12 = (bf16[1,512,192]{1,2,0:T(8,128)(2,1)S(1)}, bf16[1,512,192]{1,2,0:T(8,128)(2,1)}, u32[]{:S(2)}) copy-start(bf16[1,512,192]{1,2,0:T(8,128)(2,1)} %param.9) | copy-start | bytes 589828
  (33 other events, 46.1 us)
Sparse Core Ops, SparseCore 0:
  41.5 42.7 all-reduce.18
  86.5 19.6 all-gather.1
  121.3 42.8 all-reduce.20
  206.5 180.7 all-reduce.22
  389.7 22.1 reduce-scatter.6
  414.3 23.2 reduce-scatter.8
  440.2 125.7 all-reduce.24
